TPU v7x, 32 devices: a whole 2x2x4 slice. The times are simulated.
32 devices in a mesh: ctx: 8 (over y, x, core), head: 4 (over z).
Axes of the slice: x: 2, y: 2, z: 4, core: 2. Of those that a mesh axis runs over, the one named last changes fastest.
Arguments:
- token_ids: int32 [2048], P('ctx'), may hold values from 0 to 31999
- labels: int32 [2048], P('ctx'), may hold values from 0 to 31999
- answer_mask: int32 [2048], P('ctx'), may hold values 0 or 1
- pair_map: int32 [8], replicated, may hold values from 0 to 7, each once
- w_layer: float32 [2048, 21504], P('ctx', 'head')
- w_vocab: float32 [2048, 64000], P('ctx', 'head')
- gains: float32 [2048, 3], P('ctx'), may hold values from 0.5 to 1.5
- mom_layer: float32 [2048, 21504], P('ctx', 'head'), may hold values from -1.1444092e-05 to 1.1444092e-05
- mom_vocab: float32 [2048, 64000], P('ctx', 'head'), may hold values from -1.1444092e-05 to 1.1444092e-05
- mom_gains: float32 [2048, 3], P('ctx'), may hold values from -1.1444092e-05 to 1.1444092e-05
- avg_layer: float32 [2048, 21504], P('ctx', 'head')
- avg_vocab: float32 [2048, 64000], P('ctx', 'head')
- avg_gains: float32 [2048, 3], P('ctx'), may hold values from 0.5 to 1.5
Outputs:
- layer_new: float32 [2048, 21504], P('ctx', 'head')
- layer_moment: float32 [2048, 21504], P('ctx', 'head')
- layer_average: float32 [2048, 21504], P('ctx', 'head')
- layer_copy: bfloat16 [2048, 21504], P('ctx', 'head')
- vocab_new: float32 [2048, 64000], P('ctx', 'head')
- vocab_moment: float32 [2048, 64000], P('ctx', 'head')
- vocab_average: float32 [2048, 64000], P('ctx', 'head')
- vocab_copy: bfloat16 [2048, 64000], P('ctx', 'head')
- gains_new: float32 [2048, 3], P('ctx')
- gains_moment: float32 [2048, 3], P('ctx')
- gains_average: float32 [2048, 3], P('ctx')
- gains_copy: bfloat16 [2048, 3], P('ctx')
- loss: float32 [], replicated
- grad_norm: float32 [], replicated
Inputs may be any that keep to these rules, and one draw needn't show every extreme that they name: `pair_map`: each index of ctx appears once.
All inputs are finite; a program needn't handle non-finite values. No bound on the sum of `answer_mask` on one device may be relied on, other than what follows from the above.
Results may differ from a plain program's by a relative error of at most 0.015.
The roundings to bfloat16 on the way count: a program that leaves them out, or rounds other values in their place, can miss the bound.
Values may be sent and summed in bfloat16 or wider, within the bound.
No kernel may reach another device: no remote copies, remote signals or barrier semaphores. Data moves between devices by JAX's collectives and lax.ppermute only.
A program may use at most 832 MiB of HBM per device.

v0:
```python
import math
import jax
import jax.numpy as jnp
from jax import lax
from jax.sharding import PartitionSpec as P

D = 2048
HEADS = 32
KV = 4
HD = 64
FF = 5632
V = 32000
SEQS = 2
eps = 1e-05
z_weight = 0.0001
momentum_rate = 0.5
average_rate = 0.5
clip_level = 0.01


def merged(value, axis, join):
    pieces = jax.tree.map(lambda part: lax.all_gather(part, axis), value)
    head = jax.tree.map(lambda part: part[0], pieces)
    tail = jax.tree.map(lambda part: part[1:], pieces)
    subtotal, _ = lax.scan(lambda subtotal, share: (join(subtotal, share), None), head, tail)
    return subtotal


def widths():
    group = HEADS // KV
    return (group, group * HD, FF // KV, V // KV)


def layer_spread(length):
    group, qg, ffg, vg = widths()
    attn_in = qg + 2 * HD
    column = jnp.arange(attn_in + qg + 3 * ffg)
    return jnp.where(
        column < attn_in,
        D ** (-0.5),
        jnp.where(
            column < attn_in + qg,
            (length / (4.0 * HEADS * HD)) ** 0.5,
            jnp.where(column < attn_in + qg + 2 * ffg, D ** (-0.5), FF ** (-0.5)),
        ),
    ).astype(jnp.float32)


def vocab_spread():
    vg = V // KV
    column = jnp.arange(2 * vg)
    return jnp.where(column < vg, 2.0 * D ** (-0.5), 1.0).astype(jnp.float32)


def total_params():
    return D * (2 * HEADS * HD + 2 * KV * HD + 3 * FF + 2 * V + 3)


def yarn_tables(positions, head_dim):
    half = head_dim // 2
    index = jnp.arange(half, dtype=jnp.float32)
    inverse = 10000.0 ** (-2.0 * index / head_dim)
    ratio = 2048.0 * inverse / (2.0 * math.pi)
    ramp = jnp.clip((ratio - 1.0) / 31.0, 0.0, 1.0)
    freq = (1.0 - ramp) * inverse / 4.0 + ramp * inverse
    angle = positions[:, None] * freq[None, :]
    mscale = 0.1 * math.log(4.0) + 1.0
    return (jnp.cos(angle) * mscale, jnp.sin(angle) * mscale)


def rope(x, cosine, sine):
    half = x.shape[-1] // 2
    first = x[..., :half]
    second = x[..., half:]
    return jnp.concatenate(
        [first * cosine - second * sine, second * cosine + first * sine], axis=-1
    )


def norm(x, gain):
    return x * lax.rsqrt(jnp.mean(x * x, axis=-1, keepdims=True) + eps) * gain


def update(weight, moment, average, grad, rate):
    moment_new = momentum_rate * moment + grad
    weight_new = weight - rate * (grad + momentum_rate * moment_new)
    average_new = average_rate * average + (1.0 - average_rate) * weight_new
    return (weight_new, moment_new, average_new)


def merge_stats(first, second):
    top = jnp.maximum(first[0], second[0])
    total = first[1] * jnp.exp(first[0] - top) + second[1] * jnp.exp(second[0] - top)
    return (top, total, first[2] + second[2])


def keep_same(args):
    return args


def contract_first(left, right):
    return lax.dot_general(
        left, right, (((1,), (1,)), ((), ())), preferred_element_type=jnp.float32
    )


def masked_scores(q_part, keys, q_index, k_index, span):
    scores = jnp.einsum(
        "qhd,kd->hqk", q_part, keys, preferred_element_type=jnp.float32
    ) * keys.shape[-1] ** (-0.5)
    offset = jnp.arange(span, dtype=jnp.int32)
    allowed = (k_index * span + offset)[None, :] <= (q_index * span + offset)[:, None]
    return jnp.where(allowed[None], scores, -jnp.inf)


def local(
    token_ids,
    labels,
    answer_mask,
    pair_map,
    w_layer,
    w_vocab,
    gains,
    mom_layer,
    mom_vocab,
    mom_gains,
    avg_layer,
    avg_vocab,
    avg_gains,
):
    f32 = jnp.float32
    bf16 = jnp.bfloat16
    group, qg, ffg, vg = widths()
    attn_in = qg + 2 * HD
    layer_width = attn_in + qg + 3 * ffg
    n_ctx = lax.axis_size("ctx")
    n_head = lax.axis_size("head")
    place = lax.axis_index("ctx")
    shard = lax.axis_index("head")
    tok = token_ids.shape[0]
    nblk = 2 * SEQS
    span = tok // nblk
    length = n_ctx * tok // SEQS
    scale = HD ** (-0.5)
    first = pair_map[place]
    mirror = 2 * n_ctx - 1 - first
    local_rows = jnp.arange(tok, dtype=jnp.int32)
    positions = jnp.where(local_rows // span % 2 == 0, first, mirror) * span + local_rows % span
    cosine, sine = yarn_tables(positions.astype(f32), HD)
    vocab_send = w_vocab.astype(bf16)
    layer_full, vocab_full, gain_full = (
        lax.all_gather(w_layer.astype(bf16), "ctx", axis=0, tiled=True),
        lax.all_gather(vocab_send, "ctx", axis=0, tiled=True),
        lax.all_gather(gains.astype(bf16), "ctx", axis=0, tiled=True),
    )
    gain_f = gain_full.astype(f32)
    w_in = layer_full[:, :attn_in]
    w_out = layer_full[:, attn_in : attn_in + qg]
    w_gu = layer_full[:, attn_in + qg : attn_in + qg + 2 * ffg]
    w_down = layer_full[:, attn_in + qg + 2 * ffg :]
    w_head = vocab_full[:, :vg]
    offset_id = shard * vg
    local_ids = token_ids - offset_id
    inside = (local_ids >= 0) & (local_ids < vg)
    picked = jnp.take(vocab_full[:, vg:], jnp.where(inside, local_ids, 0), axis=1).T
    embedded = jnp.where(inside[:, None], picked, jnp.zeros_like(picked))
    x0 = lax.psum(embedded.astype(f32).astype(jnp.bfloat16), "head").astype(jnp.float32)
    a1 = norm(x0, gain_f[:, 0]).astype(bf16)
    raw = jnp.dot(a1, w_in, preferred_element_type=f32)

    def rotate(values):
        queries = rope(values[:, :qg].reshape(tok, group, HD), cosine[:, None, :], sine[:, None, :])
        keys = rope(values[:, qg : qg + HD], cosine, sine)
        return (queries, keys, values[:, qg + HD :])

    (q_f, k_f, v_f), rotate_back = jax.vjp(rotate, raw)
    q_blocks = q_f.astype(bf16).reshape(nblk, span, group, HD)
    kv_local = jnp.concatenate([k_f, v_f], axis=1).astype(bf16)
    kv_every, mask_every = (
        lax.all_gather(kv_local, "ctx", axis=0, tiled=True),
        lax.all_gather(answer_mask.astype(bf16), "ctx", axis=0, tiled=True),
    )
    count = jnp.sum(mask_every.astype(f32))
    kv_blocks = kv_every.reshape(n_ctx, nblk, span, 2 * HD)
    key_index = jnp.stack([pair_map, 2 * n_ctx - 1 - pair_map], axis=1)
    q_index = jnp.stack([first, mirror] * SEQS)

    def stat_step(carry, item):
        top, total = carry
        keys_dev, k_index = item
        for b in range(nblk):
            for half in range(2):
                kb = 2 * (b // 2) + half

                def stat_live(args):
                    top_b, total_b = args
                    s = masked_scores(
                        q_blocks[b], keys_dev[kb, :, :HD], q_index[b], k_index[half], span
                    )
                    new_top = jnp.maximum(top_b, jnp.max(s, axis=-1))
                    return (
                        new_top,
                        total_b * jnp.exp(top_b - new_top)
                        + jnp.sum(jnp.exp(s - new_top[..., None]), axis=-1),
                    )

                new = lax.cond(
                    k_index[half] <= q_index[b], stat_live, keep_same, (top[b], total[b])
                )
                top = top.at[b].set(new[0])
                total = total.at[b].set(new[1])
        return ((top, total), None)

    start_top = jnp.full((nblk, group, span), -jnp.inf, f32)
    start_total = jnp.zeros((nblk, group, span), f32)
    (top, total), _ = lax.scan(stat_step, (start_top, start_total), (kv_blocks, key_index))
    lse_attn = top + jnp.log(total)

    def out_step(acc, item):
        keys_dev, k_index = item
        for b in range(nblk):
            for half in range(2):
                kb = 2 * (b // 2) + half

                def out_live(acc_b):
                    s = masked_scores(
                        q_blocks[b], keys_dev[kb, :, :HD], q_index[b], k_index[half], span
                    )
                    probs = jnp.exp(s - lse_attn[b][..., None])
                    return acc_b + jnp.einsum(
                        "hqk,kd->hqd",
                        probs.astype(bf16),
                        keys_dev[kb, :, HD:],
                        preferred_element_type=f32,
                    )

                acc = acc.at[b].set(
                    lax.cond(k_index[half] <= q_index[b], out_live, keep_same, acc[b])
                )
        return (acc, None)

    acc, _ = lax.scan(out_step, jnp.zeros((nblk, group, span, HD), f32), (kv_blocks, key_index))
    attn_f = acc.transpose(0, 2, 1, 3).reshape(tok, qg)
    attn_b = attn_f.astype(bf16)
    y_attn = lax.psum(contract_first(attn_b, w_out).astype(jnp.bfloat16), "head").astype(
        jnp.float32
    )
    x1 = x0 + y_attn
    a2 = norm(x1, gain_f[:, 1]).astype(bf16)
    gate_up = jnp.dot(a2, w_gu, preferred_element_type=f32)

    def glu(values):
        return jax.nn.silu(values[:, :ffg]) * values[:, ffg:]

    hidden_f, glu_back = jax.vjp(glu, gate_up)
    hidden_b = hidden_f.astype(bf16)
    y_ffn = lax.psum(contract_first(hidden_b, w_down).astype(jnp.bfloat16), "head").astype(
        jnp.float32
    )
    x2 = x1 + y_ffn
    final_b = norm(x2, gain_f[:, 2]).astype(bf16)
    logits = jnp.dot(final_b, w_head, preferred_element_type=f32)
    row_top = jnp.max(logits, axis=-1)
    row_total = jnp.sum(jnp.exp(logits - row_top[:, None]), axis=-1)
    local_labels = labels - offset_id
    label_in = (local_labels >= 0) & (local_labels < vg)
    hit = (jnp.arange(vg, dtype=jnp.int32)[None, :] == local_labels[:, None]) & label_in[:, None]
    label_logit = jnp.sum(jnp.where(hit, logits, 0.0), axis=-1)
    top_all, total_all, label_all = merged((row_top, row_total, label_logit), "head", merge_stats)
    lse = top_all + jnp.log(total_all)
    valid = answer_mask.astype(f32)
    loss_part = jnp.sum(valid * (lse - label_all + z_weight * lse * lse)) / count
    soft = jnp.exp(logits - lse[:, None])
    dlog_b = (
        (valid / count)[:, None] * ((1.0 + 2.0 * z_weight * lse)[:, None] * soft - hit.astype(f32))
    ).astype(bf16)
    d_final = lax.psum(contract_first(dlog_b, w_head).astype(jnp.bfloat16), "head").astype(
        jnp.float32
    )
    _, final_back = jax.vjp(norm, x2, gain_f[:, 2])
    dx2, d_gain2 = final_back(d_final)
    dyf_b = dx2.astype(bf16)
    d_hidden = jnp.dot(dyf_b, w_down, preferred_element_type=f32)
    d_gate_up_b = glu_back(d_hidden)[0].astype(bf16)
    d_second = lax.psum(contract_first(d_gate_up_b, w_gu).astype(jnp.bfloat16), "head").astype(
        jnp.float32
    )
    _, second_back = jax.vjp(norm, x1, gain_f[:, 1])
    dx1_norm, d_gain1 = second_back(d_second)
    dx1 = dx2 + dx1_norm
    dya_b = dx1.astype(bf16)
    d_attn_b = jnp.dot(dya_b, w_out, preferred_element_type=f32).astype(bf16)
    d_blocks = d_attn_b.reshape(nblk, span, group, HD)
    delta = jnp.einsum(
        "bqhd,bqhd->bhq", d_blocks.astype(f32), attn_f.reshape(nblk, span, group, HD)
    )

    def back_step(dq, item):
        keys_dev, k_index = item
        dkv = jnp.zeros((nblk, span, 2 * HD), f32)
        for b in range(nblk):
            for half in range(2):
                kb = 2 * (b // 2) + half

                def back_live(args):
                    dq_b, dkv_b = args
                    keys = keys_dev[kb, :, :HD]
                    values = keys_dev[kb, :, HD:]
                    s = masked_scores(q_blocks[b], keys, q_index[b], k_index[half], span)
                    probs = jnp.exp(s - lse_attn[b][..., None])
                    grad_v = jnp.einsum(
                        "hqk,qhd->kd", probs.astype(bf16), d_blocks[b], preferred_element_type=f32
                    )
                    grad_p = jnp.einsum(
                        "qhd,kd->hqk", d_blocks[b], values, preferred_element_type=f32
                    )
                    grad_s = (probs * (grad_p - delta[b][..., None])).astype(bf16)
                    dq_new = dq_b + scale * jnp.einsum(
                        "hqk,kd->qhd", grad_s, keys, preferred_element_type=f32
                    )
                    grad_k = scale * jnp.einsum(
                        "hqk,qhd->kd", grad_s, q_blocks[b], preferred_element_type=f32
                    )
                    return (dq_new, dkv_b + jnp.concatenate([grad_k, grad_v], axis=-1))

                new = lax.cond(k_index[half] <= q_index[b], back_live, keep_same, (dq[b], dkv[kb]))
                dq = dq.at[b].set(new[0])
                dkv = dkv.at[kb].set(new[1])
        return (dq, dkv)

    dq, dkv_every = lax.scan(
        back_step, jnp.zeros((nblk, span, group, HD), f32), (kv_blocks, key_index)
    )
    dkv_own = lax.psum_scatter(
        dkv_every.reshape(n_ctx * tok, 2 * HD).astype(jnp.bfloat16),
        "ctx",
        scatter_dimension=0,
        tiled=True,
    ).astype(jnp.float32)
    d_raw_b = rotate_back((dq.reshape(tok, group, HD), dkv_own[:, :HD], dkv_own[:, HD:]))[0].astype(
        bf16
    )
    d_first = lax.psum(contract_first(d_raw_b, w_in).astype(jnp.bfloat16), "head").astype(
        jnp.float32
    )
    _, first_back = jax.vjp(norm, x0, gain_f[:, 0])
    dx0_norm, d_gain0 = first_back(d_first)
    dx0 = dx1 + dx0_norm
    embed_slot = jnp.where(inside, local_ids, vg)

    def outer(left, right):
        return lax.dot_general(
            left, right, (((0,), (0,)), ((), ())), preferred_element_type=jnp.float32
        )

    gain_term = jnp.stack([d_gain0, d_gain1, d_gain2], axis=1)
    parts = [
        outer(a1, d_raw_b),
        outer(dya_b, attn_b),
        outer(a2, d_gate_up_b),
        outer(dyf_b, hidden_b),
        outer(final_b, dlog_b),
    ]
    parts.append(jax.ops.segment_sum(dx0, embed_slot, vg + 1)[:vg].T)
    parts.append(gain_term)
    grads = lax.psum_scatter(
        jnp.concatenate(parts, axis=1).astype(jnp.bfloat16), "ctx", scatter_dimension=0, tiled=True
    ).astype(jnp.float32)
    grad_layer = grads[:, :layer_width]
    grad_vocab = grads[:, layer_width : layer_width + 2 * vg]
    grad_gain = grads[:, layer_width + 2 * vg :]
    squares = (
        jnp.sum(grad_layer * grad_layer)
        + jnp.sum(grad_vocab * grad_vocab)
        + jnp.sum(grad_gain * grad_gain) / n_head
    )
    total_sq, loss = lax.psum((squares, loss_part / n_head), ("ctx", "head"))
    grad_norm = jnp.sqrt(total_sq)
    factor = jnp.minimum(1.0, clip_level / grad_norm)
    base = 1.5 * math.sqrt(total_params()) / clip_level
    layer_new, layer_moment, layer_average = update(
        w_layer, mom_layer, avg_layer, factor * grad_layer, base * layer_spread(length)
    )
    vocab_new, vocab_moment, vocab_average = update(
        w_vocab, mom_vocab, avg_vocab, factor * grad_vocab, base * vocab_spread()
    )
    gains_new, gains_moment, gains_average = update(
        gains, mom_gains, avg_gains, factor * grad_gain, base * 0.1
    )
    return (
        layer_new,
        layer_moment,
        layer_average,
        layer_new.astype(bf16),
        vocab_new,
        vocab_moment,
        vocab_average,
        vocab_new.astype(bf16),
        gains_new,
        gains_moment,
        gains_average,
        gains_new.astype(bf16),
        loss,
        grad_norm,
    )


def solution(mesh):
    in_specs = (
        P("ctx"),
        P("ctx"),
        P("ctx"),
        P(),
        P("ctx", "head"),
        P("ctx", "head"),
        P("ctx", None),
        P("ctx", "head"),
        P("ctx", "head"),
        P("ctx", None),
        P("ctx", "head"),
        P("ctx", "head"),
        P("ctx", None),
    )
    out_specs = (
        P("ctx", "head"),
        P("ctx", "head"),
        P("ctx", "head"),
        P("ctx", "head"),
        P("ctx", "head"),
        P("ctx", "head"),
        P("ctx", "head"),
        P("ctx", "head"),
        P("ctx", None),
        P("ctx", None),
        P("ctx", None),
        P("ctx", None),
        P(),
        P(),
    )
    return jax.shard_map(local, mesh=mesh, in_specs=in_specs, out_specs=out_specs, check_vma=False)
```

profile of v0, /device:TPU:0, one launch (start us, length us, event | category | flops | bytes accessed | tf_op | source)
XLA Modules:
  0.0 3086.4 jit_solution(16151892121469663935)
XLA Ops:
  7.2 16.9 copy.201
  24.1 8.7 convert_element_type.296
  33.5 311.4 %all-gather.10.cloned.1.call-done = bf16[2048,16000]{0,1:T(8,128)(2,1)} async-done(((bf16[256,16000]{0,1:T(8,128)(2,1)}), bf16[2048,16000]{0,1:T(8,128)(2,1)}) %all-gather.10.cloned.1.call-update) | async-done | bytes 65536016 | tf_op jit(solution)/shard_map/all_gather | solution.py:153
  344.9 22.7 slice.1746
  367.5 10.3 gather_fusion
  379.0 4.4 convert_element_type.301
  385.4 8.9 all_gather.34
  395.1 35.7 %all-reduce.18.cloned.1.call-done = bf16[256,2048]{1,0:T(8,128)(2,1)} async-done(((bf16[256,2048]{1,0:T(8,128)(2,1)}), bf16[256,2048]{1,0:T(8,128)(2,1)}) %all-reduce.18.cloned.1.call-update) | async-done | bytes 1048592 | tf_op jit(solution)/shard_map/psum | solution.py:167
  432.3 112.1 %all-gather.12.cloned.1.call-done = bf16[2048,5376]{1,0:T(8,128)(2,1)} async-done(((bf16[256,5376]{1,0:T(8,128)(2,1)}), bf16[2048,5376]{1,0:T(8,128)(2,1)}) %all-gather.12.cloned.1.call-update) | async-done | bytes 22020112 | tf_op jit(solution)/shard_map/all_gather | solution.py:152
  550.5 10.0 all_gather.36
  560.5 118.1 %while.97 = (s32[]{:T(128)}, f32[4,8,64]{2,1,0:T(8,128)S(1)}, f32[4,8,64]{2,1,0:T(8,128)S(1)}, s32[8,2]{1,0:T(8,128)S(1)}, s32[1]{0:T(128)}, /*index=5*/bf16[8,4...) while((s32[]{:T(128)}, f32[4,8,64]{2,1,0:T(8,128)S(1)}, ...), condition=%wide.region_35.36_spmd, body=%wide.region_2.35_spmd.sunk | while | flops 34907160 | bytes 3867729 | solution.py:216
  678.7 74.8 %while.98 = (s32[]{:T(128)}, f32[4,8,64,64]{3,2,1,0:T(8,128)S(1)}, s32[8,2]{1,0:T(8,128)S(1)}, s32[1]{0:T(128)}, bf16[8,4,64,128]{3,2,1,0:T(8,128)(2,1)S(1)}, /*...) while((s32[]{:T(128)}, f32[4,8,64,64]{3,2,1,0:T(8,128)S(1)}, ...), condition=%wide.region_54.55_spmd, body=%wide.region_37.54_spmd.sunk | while | flops 68453392 | bytes 10003377 | solution.py:242
  758.3 76.2 %all-reduce.20.cloned.1.call-done = bf16[256,2048]{1,0:T(8,128)(2,1)} async-done(((bf16[256,2048]{1,0:T(8,128)(2,1)}), bf16[256,2048]{1,0:T(8,128)(2,1)}) %all-reduce.20.cloned.1.call-update) | async-done | bytes 1048592 | tf_op jit(solution)/shard_map/psum | solution.py:245
  836.3 6.4 fusion.438
  844.7 5.7 fusion.451
  850.5 9.2 all-gather.3
  860.3 41.4 %all-reduce.22.cloned.1.call-done = bf16[256,2048]{1,0:T(8,128)(2,1)} async-done(((bf16[256,2048]{1,0:T(8,128)(2,1)}), bf16[256,2048]{1,0:T(8,128)(2,1)}) %all-reduce.22.cloned.1.call-update) | async-done | bytes 1048592 | tf_op jit(solution)/shard_map/psum | solution.py:257
  903.5 18.5 fusion.534
  922.0 5.1 select_reduce_fusion
  927.1 9.3 all-gather.5
  936.3 7.9 all-gather.6
  944.3 9.2 all-gather.4
  955.0 17.9 fusion.448
  973.5 6.1 copy.219
  979.6 16.9 copy.221
  996.5 17.0 copy.223
  1013.4 6.1 copy.218
  1028.4 5.0 fusion.487
  1035.0 8.4 fusion.445
  1043.7 18.0 convolution_convert_fusion
  1063.0 31.7 %all-reduce.26.cloned.1.call-done = bf16[256,2048]{1,0:T(8,128)(2,1)} async-done(((bf16[256,2048]{1,0:T(8,128)(2,1)}), bf16[256,2048]{1,0:T(8,128)(2,1)}) %all-reduce.26.cloned.1.call-update) | async-done | bytes 1048592 | tf_op jit(solution)/shard_map/psum | solution.py:285
  1107.3 348.0 %while.100 = (s32[]{:T(128)}, f32[4,64,8,64]{3,1,2,0:T(8,128)}, bf16[8,4,64,128]{3,2,1,0:T(8,128)(2,1)}, s32[8,2]{1,0:T(8,128)S(1)}, s32[1]{0:T(128)}, /*index=5...) while((s32[]{:T(128)}, f32[4,64,8,64]{3,1,2,0:T(8,128)}, ...), condition=%wide.region_85.86_spmd, body=%wide.region_68.85_spmd.sunk | while | flops 170320912 | bytes 24750540 | solution.py:331
  1148.8 4.0 conditional.71
  1161.6 3.9 conditional.64
  1234.5 4.0 conditional.71
  1247.3 3.9 conditional.64
  1289.4 3.9 conditional.64
  1362.4 4.0 conditional.71
  1375.2 3.9 conditional.64
  1457.4 8.3 convolution_convert_fusion.1
  1465.7 15.2 copy.217
  1484.3 12.8 reduce-scatter.4.cloned.1.call-done
  1502.9 4.2 convolution_convert_fusion.2
  1511.8 43.1 %all-reduce.28.cloned.1.call-done = bf16[256,2048]{1,0:T(8,128)(2,1)} async-done(((bf16[256,2048]{1,0:T(8,128)(2,1)}), bf16[256,2048]{1,0:T(8,128)(2,1)}) %all-reduce.28.cloned.1.call-update) | async-done | bytes 1048592 | tf_op jit(solution)/shard_map/psum | solution.py:343
  1560.5 20.7 broadcast_in_dim.409
  1581.2 50.5 %scatter_fusion = f32[8001,2048]{1,0:T(8,128)} fusion(f32[8001,2048]{1,0:T(8,128)} %broadcast_in_dim.409, s32[256]{0:T(256)S(1)} %copy-done.51, f32[256,2048]{1,0:T(8,128)S(1)} %copy-done.16), kind=kCustom, calls=%fused_computation.1 | custom fusion | flops 524288 | bytes 6292480 | tf_op jit(solution)/shard_map/scatter-add | solution.py:364
  1631.7 31.9 %fusion.431 = bf16[2048,8000]{0,1:T(8,128)(2,1)} fusion(f32[8001,2048]{1,0:T(8,128)} %scatter_fusion), kind=kLoop, calls=%fused_computation.658 | loop fusion | bytes 65536000 | tf_op jit(solution)/shard_map/transpose | solution.py:364
  1663.6 352.5 %concatenate.149 = bf16[2048,21379]{0,1:T(8,128)(2,1)} concatenate(bf16[2048,640]{0,1:T(8,128)(2,1)S(1)} %copy-done.13, bf16[2048,512]{0,1:T(8,128)(2,1)} %convolution_convert_fusion.4, bf16[2048,2816]{0,1:T(8,128)(2,1)} %copy.217, bf16[2048,1408]{0,1:T(8,128)(2,1)} %convolution_convert_fusion.2, bf16[2048,8000]{0,1:T(8,128)(2,1)} %convolution_convert_fusion, ...), dimensions={1} | concatenate | bytes 175136768 | tf_op jit(solution)/shard_map/concatenate | solution.py:367
  2016.1 850.9 %reduce_scatter.22 = bf16[256,21379]{0,1:T(8,128)(2,1)} reduce-scatter(bf16[2048,21379]{0,1:T(8,128)(2,1)} %concatenate.149), channel_id=1, replica_groups=mesh['ctx'=8,'head'=4] {'ctx'}, use_global_device_ids=true, dimensions={0}, to_apply=%region_93.94 | reduce-scatter | bytes 98514432 | tf_op jit(solution)/shard_map/reduce_scatter | solution.py:366
  2867.1 6.1 convert_element_type.331
  2873.2 5.5 multiply_reduce_fusion
  2883.5 6.2 copy.220
  2889.6 38.1 %all-reduce.10 = (f32[]{:T(128)}, f32[]{:T(128)}) all-reduce(f32[]{:T(128)S(6)} %add.903, f32[]{:T(128)S(6)} %div.118), channel_id=1, replica_groups=mesh['ctx'=8,'head'=4] {'ctx','head'}, use_global_device_ids=true, to_apply=%region_97.98 | all-reduce | flops 2 | bytes 16 | tf_op jit(solution)/shard_map/psum | solution.py:377
  2929.8 29.8 fusion.519
  2959.6 16.9 copy.228
  2976.5 17.5 add_multiply_fusion
  2994.0 16.9 copy.230
  3010.8 16.9 copy.229
  3027.7 11.6 copy.231
  3039.3 9.9 fusion.520
  3049.2 6.1 copy.224
  3055.3 7.3 add_multiply_fusion.1
  3062.7 6.1 copy.226
  3068.7 6.1 copy.225
  (1843 shorter events, 649.5 us)
Async XLA Ops:
  7.2 337.7 %all-gather.10.cloned.1.call-start = ((), (), s32[]{:S(2)}) async-start(), calls=%async_computation.2 | async-start | bytes 73728000 | tf_op jit(solution)/shard_map/all_gather | solution.py:153
  32.8 397.9 %all-reduce.18.cloned.1.call-start = ((), (), s32[]{:S(2)}) async-start(), calls=%async_computation.3 | async-start | bytes 2097152 | tf_op jit(solution)/shard_map/psum | solution.py:167
  379.0 165.4 %all-gather.12.cloned.1.call-start = ((), (), s32[]{:S(2)}) async-start(), calls=%async_computation.4 | async-start | bytes 24772608 | tf_op jit(solution)/shard_map/all_gather | solution.py:152
  383.4 451.1 %all-reduce.20.cloned.1.call-start = ((), (), s32[]{:S(2)}) async-start(), calls=%async_computation.5 | async-start | bytes 2097152 | tf_op jit(solution)/shard_map/psum | solution.py:245
  394.4 153.8 %copy-start.57 = (f32[32]{0:T(128)}, f32[32]{0:T(128)S(1)}, u32[]{:S(2)}) copy-start(f32[32]{0:T(128)S(1)} %multiply_add_fusion.14) | copy-start | bytes 388
  395.0 153.2 %copy-start.47 = (f32[256]{0:T(256)}, f32[256]{0:T(256)S(1)}, u32[]{:S(2)}) copy-start(f32[256]{0:T(256)S(1)} %fusion.509) | copy-start | bytes 3076
  395.0 149.4 %copy-start.36 = (f32[2048,1]{0,1:T(1,128)}, f32[2048,1]{0,1:T(1,128)S(1)}, u32[]{:S(2)}) copy-start(f32[2048,1]{0,1:T(1,128)S(1)} %get-tuple-element.2405) | copy-start | bytes 24580
  395.1 702.7 %copy-start.34 = (f32[2048,1]{0,1:T(1,128)}, f32[2048,1]{0,1:T(1,128)S(1)}, u32[]{:S(2)}) copy-start(f32[2048,1]{0,1:T(1,128)S(1)} %get-tuple-element.2403) | copy-start | bytes 24580
  432.3 112.2 %copy-start.49 = (f32[256]{0:T(256)}, f32[256]{0:T(256)S(1)}, u32[]{:S(2)}) copy-start(f32[256]{0:T(256)S(1)} %fusion.471) | copy-start | bytes 3076
  432.3 112.1 %copy-start.40 = (f32[256]{0:T(256)}, f32[256]{0:T(256)S(1)}, u32[]{:S(2)}) copy-start(f32[256]{0:T(256)S(1)} %fusion.513) | copy-start | bytes 3076
  753.5 4.7 copy-start.20
  754.8 3.5 copy-start.28
  754.8 79.7 %copy-start.1 = (bf16[256,2048]{1,0:T(8,128)(2,1)S(1)}, bf16[256,2048]{1,0:T(8,128)(2,1)}, u32[]{:S(2)}) copy-start(bf16[256,2048]{1,0:T(8,128)(2,1)} %all-reduce.18.cloned.1.call-done) | copy-start | bytes 3145732
  758.3 143.4 %all-reduce.22.cloned.1.call-start = ((), (), s32[]{:S(2)}) async-start(), calls=%async_computation.6 | async-start | bytes 2097152 | tf_op jit(solution)/shard_map/psum | solution.py:257
  836.3 261.5 %copy-start.39 = (f32[256]{0:T(256)}, f32[256]{0:T(256)S(1)}, u32[]{:S(2)}) copy-start(f32[256]{0:T(256)S(1)} %fusion.514) | copy-start | bytes 3076
  844.6 5.7 copy-start.24
  844.7 5.8 copy-start.60
  844.7 15.6 copy-start.59
  850.4 172.7 %all-reduce.24.cloned.1.call-start = ((), (), s32[]{:S(2)}) async-start(), calls=%async_computation.7 | async-start | bytes 2097152 | tf_op jit(solution)/shard_map/psum | solution.py:277
  972.9 121.8 %all-reduce.26.cloned.1.call-start = ((), (), s32[]{:S(2)}) async-start(), calls=%async_computation.8 | async-start | bytes 2097152 | tf_op jit(solution)/shard_map/psum | solution.py:285
  1023.1 3.4 copy-start.9
  1023.1 3.4 copy-start.14
  1028.4 5.1 copy-start.17
  1043.5 453.6 %reduce-scatter.4.cloned.1.call-start = ((), (), s32[]{:S(2)}) async-start(), calls=%async_computation.9 | async-start | bytes 589824 | tf_op jit(solution)/shard_map/reduce_scatter | solution.py:334
  1094.8 3.0 copy-start.15
  1094.8 3.0 copy-start.21
  1107.3 8.1 copy-start.53
  1147.4 10.0 copy-start.54
  1157.4 8.2 copy-start.53
  1193.6 5.9 copy-start.54
  1199.5 4.9 copy-start.53
  1233.1 10.0 copy-start.54
  1243.1 8.2 copy-start.53
  1279.3 5.9 copy-start.54
  1285.2 8.2 copy-start.53
  1321.5 5.9 copy-start.54
  1327.4 4.9 copy-start.53
  1361.0 10.0 copy-start.54
  1371.0 8.2 copy-start.53
  1407.2 5.9 copy-start.54
  1413.1 8.2 copy-start.53
  1449.3 5.9 copy-start.54
  1457.3 97.6 %all-reduce.28.cloned.1.call-start = ((), (), s32[]{:S(2)}) async-start(), calls=%async_computation.10 | async-start | bytes 2097152 | tf_op jit(solution)/shard_map/psum | solution.py:343
  1465.7 15.3 copy-start.43
  1465.7 15.3 copy-start.5
  1480.9 3.2 copy-start.31
  1480.9 3.2 copy-start.33
  1482.3 15.6 copy-start.48
  1482.3 15.6 copy-start.58
  1498.9 3.9 copy-start.18
  1498.9 3.9 copy-start.25
  1502.9 4.3 copy-start.42
  1502.9 4.3 copy-start.7
  1502.9 4.3 copy-start.29
  1511.7 45.6 %copy-start.50 = (f32[256]{0:T(256)S(1)}, f32[256]{0:T(256)}, u32[]{:S(2)}) copy-start(f32[256]{0:T(256)} %copy-done.49) | copy-start | bytes 3076
  1560.5 20.7 copy-start.16
  1560.5 20.7 copy-start.51
  1631.7 31.9 %copy-start.13 = (bf16[2048,640]{0,1:T(8,128)(2,1)S(1)}, bf16[2048,640]{0,1:T(8,128)(2,1)}, u32[]{:S(2)}) copy-start(bf16[2048,640]{0,1:T(8,128)(2,1)} %convolution_convert_fusion.3) | copy-start | bytes 7864324
  2873.2 7.7 copy-start
  2883.4 45.0 %copy-start.46 = (f32[256,3]{0,1:T(4,128)S(1)}, f32[256,3]{0,1:T(4,128)}, u32[]{:S(2)}) copy-start(f32[256,3]{0,1:T(4,128)} %param.155) | copy-start | bytes 9220
  2883.4 45.0 %copy-start.56 = (f32[256,3]{0,1:T(4,128)S(1)}, f32[256,3]{0,1:T(4,128)}, u32[]{:S(2)}) copy-start(f32[256,3]{0,1:T(4,128)} %param.158) | copy-start | bytes 9220
  2883.5 46.3 %copy-start.35 = (f32[16000]{0:T(1024)S(1)}, f32[16000]{0:T(1024)}, u32[]{:S(2)}) copy-start(f32[16000]{0:T(1024)} %select_multiply_fusion) | copy-start | bytes 192004
  2929.8 147.9 %copy-start.44 = (f32[256,3]{0,1:T(4,128)}, f32[256,3]{0,1:T(4,128)S(1)}, u32[]{:S(2)}) copy-start(f32[256,3]{0,1:T(4,128)S(1)} %get-tuple-element.2287) | copy-start | bytes 9220
  3027.7 11.6 copy-start.38
  (35 other events, 50.6 us)
Sparse Core Ops, SparseCore 0:
  32.9 311.8 all-gather.9
  379.1 51.5 all-reduce.17
  433.2 111.1 all-gather.11
  758.4 76.0 all-reduce.19
  850.5 51.1 all-reduce.21
  973.1 50.0 all-reduce.23
  1043.6 51.1 all-reduce.25
  1457.5 39.5 reduce-scatter.3
  1503.0 51.8 all-reduce.27
where the time goes:
time: 3120 us; the launch traced here: 3090 us
  blocking collectives  944 us (30%)
  local copies, waits for them, and re-layouts  923 us (30%)
  waiting for transfers between devices  666 us (21%)
  other arithmetic  203 us (7%)
  matrix products  175 us (6%)
  loops' own time  153 us (5%)
    reduce_scatter x1, blocking collectives, local(): lax.psum_scatter(jnp.concatenate(parts, axis=1).astype(jnp.bfloat16), 'ct...  851 us
    concatenate x1, local copies, waits for them, and re-layouts, local(): jnp.concatenate(parts, axis=1).astype(jnp.bfloat16)  353 us
    all_gather x1, waiting for transfers between devices, local(): lax.all_gather(vocab_send, 'ctx', axis=0, tiled=True)  311 us
    unnamed x136, local copies, waits for them, and re-layouts  161 us
    all_gather x1, waiting for transfers between devices, local(): lax.all_gather(w_layer.astype(bf16), 'ctx', axis=0, tiled=True)  112 us
    psum x1, waiting for transfers between devices, local(): lax.psum(contract_first(attn_b, w_out).astype(jnp.bfloat16), 'head')  76.2 us
    scatter x64, local copies, waits for them, and re-layouts, back_step(): dq = dq.at[b].set(new[0])  68.9 us
  transfers between devices with their start and end apart: 9, of which 9 were waited for; matrix products, arithmetic and copies ran while one was open for 4% of the time, Pallas kernels for 0%

commit v1 on v0

--- a/solution.py
+++ b/solution.py
@@ -16,6 +16,32 @@
 momentum_rate = 0.5
 average_rate = 0.5
 clip_level = 0.01
+
+
+def pass_tables(body, across="ctx"):
+    sheets = []
+    j = 0
+    n = jax.lax.axis_size(across)
+    while j < n:
+        sheets.append((j, (j + 1) % n))
+        j += 1
+    heap = []
+    j = 0
+    while j < n:
+        heap.append((j, (j - 1) % n))
+        j = j + 1
+    current_value, then = ([body], [body])
+    for _ in range(n // 2):
+        a_next = jax.lax.ppermute(current_value[-1], across, sheets)
+        current_value.append(a_next)
+    dev_i = 0
+    while dev_i < (n - 1) // 2:
+        g_now = jax.lax.ppermute(then[-1], across, heap)
+        then.append(g_now)
+        dev_i += 1
+    even = jnp.concatenate([*current_value[::-1], *then[1:]], 0)
+    current_arr = jax.lax.axis_index(across)
+    return jnp.roll(even, (current_arr - n // 2) * body.shape[0], 0)
 
 
 def merged(value, axis, join):
@@ -150,7 +176,7 @@
     vocab_send = w_vocab.astype(bf16)
     layer_full, vocab_full, gain_full = (
         lax.all_gather(w_layer.astype(bf16), "ctx", axis=0, tiled=True),
-        lax.all_gather(vocab_send, "ctx", axis=0, tiled=True),
+        pass_tables(vocab_send),
         lax.all_gather(gains.astype(bf16), "ctx", axis=0, tiled=True),
     )
     gain_f = gain_full.astype(f32)

time: 3120 us -> 3550 us (1.14)
  waiting for transfers between devices: 666 us -> 923 us
  local copies, waits for them, and re-layouts: 923 us -> 1070 us
    ppermute x0 -> x7, waiting for transfers between devices: none -> 620 us  [the longest x4 620 us: pass_tables(): a_next = jax.lax.ppermute(current_value[-1], across, sheets)]
    all_gather x1 -> x0, waiting for transfers between devices: 311 us -> none  [local(): lax.all_gather(vocab_send, 'ctx', axis=0, tiled=True)]
    unnamed x136 -> x157, local copies, waits for them, and re-layouts: 161 us -> 251 us
    all_gather x1, waiting for transfers between devices: 112 us -> 62.4 us  [local(): lax.all_gather(w_layer.astype(bf16), 'ctx', axis=0, tiled=True)]
  transfers between devices with their start and end apart: 9 -> 15, of which waited for: 9 -> 12; matrix products, arithmetic and copies ran while one was open for 4% -> 4% of each run, Pallas kernels for 0% -> 0%
where the time goes in v1:
time: 3550 us; the launch traced here: 3510 us
  local copies, waits for them, and re-layouts  1070 us (30%)
  blocking collectives  943 us (27%)
  waiting for transfers between devices  923 us (26%)
  other arithmetic  215 us (6%)
  matrix products  177 us (5%)
  loops' own time  155 us (4%)
    reduce_scatter x1, blocking collectives, local(): lax.psum_scatter(jnp.concatenate(parts, axis=1).astype(jnp.bfloat16), 'ct...  851 us
    ppermute x4, waiting for transfers between devices, pass_tables(): a_next = jax.lax.ppermute(current_value[-1], across, sheets)  620 us
    concatenate x1, local copies, waits for them, and re-layouts, local(): jnp.concatenate(parts, axis=1).astype(jnp.bfloat16)  353 us
    unnamed x157, local copies, waits for them, and re-layouts  251 us
    psum x1, waiting for transfers between devices, local(): lax.psum(contract_first(attn_b, w_out).astype(jnp.bfloat16), 'head')  75.6 us
  transfers between devices with their start and end apart: 15, of which 12 were waited for; matrix products, arithmetic and copies ran while one was open for 4% of the time, Pallas kernels for 0%

profile of v1, /device:TPU:0, one launch (start us, length us, event | category | flops | bytes accessed | tf_op | source)
XLA Modules:
  0.0 3514.0 jit_solution(10518342720331383386)
XLA Ops:
  8.1 16.9 copy.201
  24.9 6.2 convert_element_type.296
  31.7 91.9 %collective-permute-done = bf16[256,16000]{0,1:T(8,128)(2,1)S(1)} collective-permute-done((bf16[256,16000]{0,1:T(8,128)(2,1)S(1)}, bf16[256,16000]{0,1:T(8,128)(2,1)S(1)}, u32[]{:S(2)}, u32[]{:S(2)}) %collective-permute-start) | collective-permute-done | bytes 8192032 | tf_op jit(solution)/shard_map/ppermute | solution.py:35
  129.6 175.1 %collective-permute-done.1 = bf16[256,16000]{0,1:T(8,128)(2,1)S(1)} collective-permute-done((bf16[256,16000]{0,1:T(8,128)(2,1)S(1)}, bf16[256,16000]{0,1:T(8,128)(2,1)S(1)}, u32[]{:S(2)}, u32[]{:S(2)}) %collective-permute-start.1) | collective-permute-done | bytes 8192032 | tf_op jit(solution)/shard_map/ppermute | solution.py:35
  310.7 176.8 %collective-permute-done.2 = bf16[256,16000]{0,1:T(8,128)(2,1)} collective-permute-done((bf16[256,16000]{0,1:T(8,128)(2,1)S(1)}, bf16[256,16000]{0,1:T(8,128)(2,1)}, u32[]{:S(2)}, u32[]{:S(2)}) %collective-permute-start.2) | collective-permute-done | bytes 8192032 | tf_op jit(solution)/shard_map/ppermute | solution.py:35
  490.2 176.5 %collective-permute-done.3 = bf16[256,16000]{0,1:T(8,128)(2,1)} collective-permute-done((bf16[256,16000]{0,1:T(8,128)(2,1)}, bf16[256,16000]{0,1:T(8,128)(2,1)}, u32[]{:S(2)}, u32[]{:S(2)}) %collective-permute-start.3) | collective-permute-done | bytes 8192032 | tf_op jit(solution)/shard_map/ppermute | solution.py:35
  666.7 7.2 constant_dynamic-update-slice_fusion.50
  674.0 8.0 constant_dynamic-update-slice_fusion.49
  698.5 7.0 constant_dynamic-update-slice_fusion.45
  705.4 7.0 constant_dynamic-update-slice_fusion.44
  712.5 7.0 constant_dynamic-update-slice_fusion.43
  719.5 7.0 constant_dynamic-update-slice_fusion.42
  726.4 7.0 constant_dynamic-update-slice_fusion.41
  744.6 7.0 constant_dynamic-update-slice_fusion.37
  751.5 7.0 constant_dynamic-update-slice_fusion.36
  758.5 7.1 constant_dynamic-update-slice_fusion.35
  765.6 22.7 dynamic-slice.358
  788.3 10.3 gather_fusion
  806.4 7.4 all_gather.30
  814.6 34.7 all-reduce.18.cloned.1.call-done
  851.1 62.4 %all-gather.9.cloned.1.call-done = bf16[2048,5376]{1,0:T(8,128)(2,1)} async-done(((bf16[256,5376]{1,0:T(8,128)(2,1)}), bf16[2048,5376]{1,0:T(8,128)(2,1)}) %all-gather.9.cloned.1.call-update) | async-done | bytes 22020112 | tf_op jit(solution)/shard_map/all_gather | solution.py:178
  919.4 11.3 all_gather.32
  930.7 136.4 %while.97 = (s32[]{:T(128)}, f32[4,8,64]{2,1,0:T(8,128)S(1)}, f32[4,8,64]{2,1,0:T(8,128)S(1)}, s32[8,2]{1,0:T(8,128)}, s32[1]{0:T(128)}, /*index=5*/bf16[8,4,64,...) while((s32[]{:T(128)}, f32[4,8,64]{2,1,0:T(8,128)S(1)}, ...), condition=%wide.region_35.36_spmd, body=%wide.region_2.35_spmd.sunk | while | flops 34907160 | bytes 3867729 | solution.py:242
  1067.2 93.0 %while.98 = (s32[]{:T(128)}, f32[4,8,64,64]{3,2,1,0:T(8,128)S(1)}, s32[8,2]{1,0:T(8,128)}, s32[1]{0:T(128)}, bf16[8,4,64,128]{3,2,1,0:T(8,128)(2,1)}, /*index=5*...) while((s32[]{:T(128)}, f32[4,8,64,64]{3,2,1,0:T(8,128)S(1)}, ...), condition=%wide.region_54.55_spmd, body=%wide.region_37.54_spmd.sunk | while | flops 68453392 | bytes 10003377 | solution.py:268
  1166.4 75.6 %all-reduce.20.cloned.1.call-done = bf16[256,2048]{1,0:T(8,128)(2,1)} async-done(((bf16[256,2048]{1,0:T(8,128)(2,1)}), bf16[256,2048]{1,0:T(8,128)(2,1)}) %all-reduce.20.cloned.1.call-update) | async-done | bytes 1048592 | tf_op jit(solution)/shard_map/psum | solution.py:271
  1243.7 6.7 fusion.438
  1258.5 9.1 all-gather.3
  1268.2 41.5 %all-reduce.22.cloned.1.call-done = bf16[256,2048]{1,0:T(8,128)(2,1)} async-done(((bf16[256,2048]{1,0:T(8,128)(2,1)}), bf16[256,2048]{1,0:T(8,128)(2,1)}) %all-reduce.22.cloned.1.call-update) | async-done | bytes 1048592 | tf_op jit(solution)/shard_map/psum | solution.py:283
  1311.5 18.5 fusion.536
  1335.1 9.3 all-gather.5
  1344.4 7.9 all-gather.6
  1352.3 9.3 all-gather.4
  1363.1 18.7 fusion.448
  1382.1 6.1 copy.219
  1388.2 16.9 copy.221
  1405.1 16.9 copy.223
  1422.0 6.1 copy.218
  1444.6 8.5 fusion.445
  1453.6 18.0 convolution_convert_fusion
  1472.9 31.5 all-reduce.26.cloned.1.call-done
  1519.7 360.6 %while.100 = (s32[]{:T(128)}, f32[4,64,8,64]{3,1,2,0:T(8,128)}, bf16[8,4,64,128]{3,2,1,0:T(8,128)(2,1)}, s32[8,2]{1,0:T(8,128)}, s32[1]{0:T(128)}, /*index=5*/bf...) while((s32[]{:T(128)}, f32[4,64,8,64]{3,1,2,0:T(8,128)}, ...), condition=%wide.region_85.86_spmd, body=%wide.region_68.85_spmd.sunk | while | flops 170320912 | bytes 24749972 | solution.py:357
  1882.5 8.3 convolution_convert_fusion.1
  1890.7 15.2 copy.217
  1909.8 11.6 reduce-scatter.4.cloned.1.call-done
  1936.2 43.1 %all-reduce.28.cloned.1.call-done = bf16[256,2048]{1,0:T(8,128)(2,1)} async-done(((bf16[256,2048]{1,0:T(8,128)(2,1)}), bf16[256,2048]{1,0:T(8,128)(2,1)}) %all-reduce.28.cloned.1.call-update) | async-done | bytes 1048592 | tf_op jit(solution)/shard_map/psum | solution.py:369
  1985.3 20.7 broadcast_in_dim.409
  2006.1 49.8 %scatter_fusion = f32[8001,2048]{1,0:T(8,128)} fusion(f32[8001,2048]{1,0:T(8,128)} %broadcast_in_dim.409, s32[256]{0:T(256)S(1)} %copy-done.46, f32[256,2048]{1,0:T(8,128)S(1)} %copy-done.12), kind=kCustom, calls=%fused_computation.1 | custom fusion | flops 524288 | bytes 6292480 | tf_op jit(solution)/shard_map/scatter-add | solution.py:390
  2055.8 31.9 fusion.431
  2087.7 353.4 %concatenate.156 = bf16[2048,21379]{0,1:T(8,128)(2,1)} concatenate(bf16[2048,640]{0,1:T(8,128)(2,1)} %convolution_convert_fusion.3, bf16[2048,512]{0,1:T(8,128)(2,1)S(1)} %copy-done.11, bf16[2048,2816]{0,1:T(8,128)(2,1)} %copy.217, bf16[2048,1408]{0,1:T(8,128)(2,1)} %convolution_convert_fusion.2, bf16[2048,8000]{0,1:T(8,128)(2,1)} %convolution_convert_fusion, ...), dimensions={1} | concatenate | bytes 175136768 | tf_op jit(solution)/shard_map/concatenate | solution.py:393
  2441.1 850.8 %reduce_scatter.22 = bf16[256,21379]{0,1:T(8,128)(2,1)} reduce-scatter(bf16[2048,21379]{0,1:T(8,128)(2,1)} %concatenate.156), channel_id=1, replica_groups=mesh['ctx'=8,'head'=4] {'ctx'}, use_global_device_ids=true, dimensions={0}, to_apply=%region_93.94 | reduce-scatter | bytes 98514432 | tf_op jit(solution)/shard_map/reduce_scatter | solution.py:392
  3292.0 6.1 convert_element_type.331
  3308.4 6.2 copy.220
  3314.5 38.3 %all-reduce.10 = (f32[]{:T(128)}, f32[]{:T(128)}) all-reduce(f32[]{:T(128)S(6)} %add.916, f32[]{:T(128)S(6)} %div.118), channel_id=1, replica_groups=mesh['ctx'=8,'head'=4] {'ctx','head'}, use_global_device_ids=true, to_apply=%region_97.98 | all-reduce | flops 2 | bytes 16 | tf_op jit(solution)/shard_map/psum | solution.py:403
  3354.9 29.8 fusion.521
  3384.7 16.9 copy.228
  3401.6 17.5 add_multiply_fusion
  3419.1 16.9 copy.230
  3436.0 16.9 copy.229
  3452.8 11.6 copy.231
  3464.5 10.1 fusion.522
  3474.6 6.1 copy.224
  3480.6 7.3 add_multiply_fusion.1
  3488.0 6.1 copy.226
  3494.1 6.1 copy.225
  (1849 shorter events, 807.5 us)
Async XLA Ops:
  8.0 841.2 %all-reduce.18.cloned.1.call-start = ((), (), s32[]{:S(2)}) async-start(), calls=%async_computation.2 | async-start | bytes 2097152 | tf_op jit(solution)/shard_map/psum | solution.py:193
  24.9 462.6 %copy-start.48 = (s32[256]{0:T(256)S(1)}, s32[256]{0:T(256)}, u32[]{:S(2)}) copy-start(s32[256]{0:T(256)} %param.149) | copy-start | bytes 3076
  31.2 92.4 %collective-permute-start = (bf16[256,16000]{0,1:T(8,128)(2,1)S(1)}, bf16[256,16000]{0,1:T(8,128)(2,1)S(1)}, u32[]{:S(2)}, u32[]{:S(2)}) collective-permute-start(bf16[256,16000]{0,1:T(8,128)(2,1)S(1)} %convert_element_type.296), channel_id=1, source_target_pairs={{0,4},{4,8},{8,12},{12,16},{16,20},{20,24},{24,28},{28,0},{1,5},{5... | collective-permute-start | bytes 24576008 | tf_op jit(solution)/shard_map/ppermute | solution.py:35
  127.0 177.7 %collective-permute-start.1 = (bf16[256,16000]{0,1:T(8,128)(2,1)S(1)}, bf16[256,16000]{0,1:T(8,128)(2,1)S(1)}, u32[]{:S(2)}, u32[]{:S(2)}) collective-permute-start(bf16[256,16000]{0,1:T(8,128)(2,1)S(1)} %collective-permute-done), channel_id=1, source_target_pairs={{0,4},{4,8},{8,12},{12,16},{16,20},{20,24},{24,28},{28,0},{1,5},{5... | collective-permute-start | bytes 24576008 | tf_op jit(solution)/shard_map/ppermute | solution.py:35
  127.0 181.1 %collective-permute-start.4 = (bf16[256,16000]{0,1:T(8,128)(2,1)S(1)}, bf16[256,16000]{0,1:T(8,128)(2,1)}, u32[]{:S(2)}, u32[]{:S(2)}) collective-permute-start(bf16[256,16000]{0,1:T(8,128)(2,1)S(1)} %convert_element_type.296), channel_id=1, source_target_pairs={{0,28},{4,0},{8,4},{12,8},{16,12},{20,16},{24,20},{28,24},{1,29},{... | collective-permute-start | bytes 24576008 | tf_op jit(solution)/shard_map/ppermute | solution.py:39
  308.0 179.5 %collective-permute-start.2 = (bf16[256,16000]{0,1:T(8,128)(2,1)S(1)}, bf16[256,16000]{0,1:T(8,128)(2,1)}, u32[]{:S(2)}, u32[]{:S(2)}) collective-permute-start(bf16[256,16000]{0,1:T(8,128)(2,1)S(1)} %collective-permute-done.1), channel_id=1, source_target_pairs={{0,4},{4,8},{8,12},{12,16},{16,20},{20,24},{24,28},{28,0},{1,5},{5... | collective-permute-start | bytes 24576008 | tf_op jit(solution)/shard_map/ppermute | solution.py:35
  308.0 179.5 %collective-permute-start.5 = (bf16[256,16000]{0,1:T(8,128)(2,1)}, bf16[256,16000]{0,1:T(8,128)(2,1)}, u32[]{:S(2)}, u32[]{:S(2)}) collective-permute-start(bf16[256,16000]{0,1:T(8,128)(2,1)} %collective-permute-done.4), channel_id=1, source_target_pairs={{0,28},{4,0},{8,4},{12,8},{16,12},{20,16},{24,20},{28,24},{1,29},{... | collective-permute-start | bytes 24576008 | tf_op jit(solution)/shard_map/ppermute | solution.py:39
  487.5 179.2 %collective-permute-start.3 = (bf16[256,16000]{0,1:T(8,128)(2,1)}, bf16[256,16000]{0,1:T(8,128)(2,1)}, u32[]{:S(2)}, u32[]{:S(2)}) collective-permute-start(bf16[256,16000]{0,1:T(8,128)(2,1)} %collective-permute-done.2), channel_id=1, source_target_pairs={{0,4},{4,8},{8,12},{12,16},{16,20},{20,24},{24,28},{28,0},{1,5},{5... | collective-permute-start | bytes 24576008 | tf_op jit(solution)/shard_map/ppermute | solution.py:35
  487.5 224.9 %collective-permute-start.6 = (bf16[256,16000]{0,1:T(8,128)(2,1)}, bf16[256,16000]{0,1:T(8,128)(2,1)}, u32[]{:S(2)}, u32[]{:S(2)}) collective-permute-start(bf16[256,16000]{0,1:T(8,128)(2,1)} %collective-permute-done.5), channel_id=1, source_target_pairs={{0,28},{4,0},{8,4},{12,8},{16,12},{20,16},{24,20},{28,24},{1,29},{... | collective-permute-start | bytes 24576008 | tf_op jit(solution)/shard_map/ppermute | solution.py:39
  666.7 15.2 slice-start.6
  674.0 8.0 slice-start.7
  674.0 12.3 slice-start.4
  682.0 4.5 slice-start.5
  682.0 8.7 slice-start
  682.0 10.3 slice-start.1
  686.5 7.1 slice-start.2
  686.5 8.2 slice-start.3
  799.9 4.5 copy-start.40
  799.9 4.5 copy-start.55
  799.9 113.7 %all-gather.9.cloned.1.call-start = ((), (), s32[]{:S(2)}) async-start(), calls=%async_computation.3 | async-start | bytes 24772608 | tf_op jit(solution)/shard_map/all_gather | solution.py:178
  804.3 437.7 %all-reduce.20.cloned.1.call-start = ((), (), s32[]{:S(2)}) async-start(), calls=%async_computation.4 | async-start | bytes 2097152 | tf_op jit(solution)/shard_map/psum | solution.py:271
  813.8 103.8 %copy-start.51 = (f32[32]{0:T(128)}, f32[32]{0:T(128)S(1)}, u32[]{:S(2)}) copy-start(f32[32]{0:T(128)S(1)} %multiply_add_fusion.14) | copy-start | bytes 388
  814.5 103.1 %copy-start.42 = (f32[256]{0:T(256)}, f32[256]{0:T(256)S(1)}, u32[]{:S(2)}) copy-start(f32[256]{0:T(256)S(1)} %fusion.509) | copy-start | bytes 3076
  814.5 102.3 %copy-start.31 = (f32[2048,1]{0,1:T(1,128)}, f32[2048,1]{0,1:T(1,128)S(1)}, u32[]{:S(2)}) copy-start(f32[2048,1]{0,1:T(1,128)S(1)} %get-tuple-element.2405) | copy-start | bytes 24580
  814.5 692.7 %copy-start.29 = (f32[2048,1]{0,1:T(1,128)}, f32[2048,1]{0,1:T(1,128)S(1)}, u32[]{:S(2)}) copy-start(f32[2048,1]{0,1:T(1,128)S(1)} %get-tuple-element.2403) | copy-start | bytes 24580
  851.1 65.7 %copy-start.44 = (f32[256]{0:T(256)}, f32[256]{0:T(256)S(1)}, u32[]{:S(2)}) copy-start(f32[256]{0:T(256)S(1)} %fusion.471) | copy-start | bytes 3076
  851.1 65.7 %copy-start.35 = (f32[256]{0:T(256)}, f32[256]{0:T(256)S(1)}, u32[]{:S(2)}) copy-start(f32[256]{0:T(256)S(1)} %fusion.513) | copy-start | bytes 3076
  1160.3 90.2 %copy-start.3 = (f32[4,8,64,64]{3,2,1,0:T(8,128)}, f32[4,8,64,64]{3,2,1,0:T(8,128)S(1)}, u32[]{:S(2)}) copy-start(f32[4,8,64,64]{3,2,1,0:T(8,128)S(1)} %get-tuple-element.1947) | copy-start | bytes 1572868
  1160.3 81.7 %copy-start.1 = (bf16[256,2048]{1,0:T(8,128)(2,1)S(1)}, bf16[256,2048]{1,0:T(8,128)(2,1)}, u32[]{:S(2)}) copy-start(bf16[256,2048]{1,0:T(8,128)(2,1)} %all-reduce.18.cloned.1.call-done) | copy-start | bytes 3145732
  1162.9 87.5 %copy-start.23 = (bf16[256,512]{1,0:T(8,128)(2,1)}, bf16[256,512]{1,0:T(8,128)(2,1)S(1)}, u32[]{:S(2)}) copy-start(bf16[256,512]{1,0:T(8,128)(2,1)S(1)} %convert_element_type.307) | copy-start | bytes 786436
  1166.3 143.4 %all-reduce.22.cloned.1.call-start = ((), (), s32[]{:S(2)}) async-start(), calls=%async_computation.5 | async-start | bytes 2097152 | tf_op jit(solution)/shard_map/psum | solution.py:283
  1243.7 263.5 %copy-start.34 = (f32[256]{0:T(256)}, f32[256]{0:T(256)S(1)}, u32[]{:S(2)}) copy-start(f32[256]{0:T(256)S(1)} %fusion.514) | copy-start | bytes 3076
  1252.9 5.6 copy-start.54
  1252.9 15.3 copy-start.53
  1252.9 56.9 %copy-start.2 = (bf16[256,2048]{1,0:T(8,128)(2,1)S(1)}, bf16[256,2048]{1,0:T(8,128)(2,1)}, u32[]{:S(2)}) copy-start(bf16[256,2048]{1,0:T(8,128)(2,1)} %all-reduce.20.cloned.1.call-done) | copy-start | bytes 3145732
  1258.5 173.6 %all-reduce.24.cloned.1.call-start = ((), (), s32[]{:S(2)}) async-start(), calls=%async_computation.6 | async-start | bytes 2097152 | tf_op jit(solution)/shard_map/psum | solution.py:303
  1381.8 122.6 %all-reduce.26.cloned.1.call-start = ((), (), s32[]{:S(2)}) async-start(), calls=%async_computation.7 | async-start | bytes 2097152 | tf_op jit(solution)/shard_map/psum | solution.py:311
  1422.0 6.7 copy-start.49
  1432.0 6.0 copy-start.17
  1438.0 5.1 copy-start.13
  1453.1 468.3 %reduce-scatter.4.cloned.1.call-start = ((), (), s32[]{:S(2)}) async-start(), calls=%async_computation.8 | async-start | bytes 589824 | tf_op jit(solution)/shard_map/reduce_scatter | solution.py:360
  1882.4 96.9 %all-reduce.28.cloned.1.call-start = ((), (), s32[]{:S(2)}) async-start(), calls=%async_computation.9 | async-start | bytes 2097152 | tf_op jit(solution)/shard_map/psum | solution.py:369
  1890.7 15.2 copy-start.38
  1890.7 15.3 copy-start.4
  1890.7 17.1 copy-start.26
  1890.7 17.1 copy-start.28
  1906.0 16.3 copy-start.43
  1906.0 16.3 copy-start.52
  1906.4 20.9 copy-start.14
  1907.8 19.5 copy-start.19
  1927.3 6.4 copy-start.20
  1927.3 6.4 copy-start.32
  1927.3 6.4 copy-start.36
  1931.6 50.0 %copy-start.45 = (f32[256]{0:T(256)S(1)}, f32[256]{0:T(256)}, u32[]{:S(2)}) copy-start(f32[256]{0:T(256)} %copy-done.44) | copy-start | bytes 3076
  1985.3 20.7 copy-start.12
  1985.3 20.7 copy-start.46
  2055.8 31.9 copy-start.11
  3298.1 7.7 copy-start
  3308.3 45.2 %copy-start.41 = (f32[256,3]{0,1:T(4,128)S(1)}, f32[256,3]{0,1:T(4,128)}, u32[]{:S(2)}) copy-start(f32[256,3]{0,1:T(4,128)} %param.155) | copy-start | bytes 9220
  3308.3 45.2 %copy-start.50 = (f32[256,3]{0,1:T(4,128)S(1)}, f32[256,3]{0,1:T(4,128)}, u32[]{:S(2)}) copy-start(f32[256,3]{0,1:T(4,128)} %param.158) | copy-start | bytes 9220
  3308.4 46.5 %copy-start.30 = (f32[16000]{0:T(1024)S(1)}, f32[16000]{0:T(1024)}, u32[]{:S(2)}) copy-start(f32[16000]{0:T(1024)} %select_multiply_fusion) | copy-start | bytes 192004
  3354.9 149.8 %copy-start.39 = (f32[256,3]{0,1:T(4,128)}, f32[256,3]{0,1:T(4,128)S(1)}, u32[]{:S(2)}) copy-start(f32[256,3]{0,1:T(4,128)S(1)} %get-tuple-element.2287) | copy-start | bytes 9220
  3452.8 11.6 copy-start.33
  3500.1 4.5 copy-start.47
  (29 other events, 50.9 us)
Sparse Core Ops, SparseCore 0:
  800.0 49.2 all-reduce.17
  1166.4 75.5 all-reduce.19
  1258.6 51.1 all-reduce.21
  1382.0 50.0 all-reduce.23
  1453.2 51.1 all-reduce.25
  1927.4 51.8 all-reduce.27
Sparse Core Ops, SparseCore 1:
  804.4 109.1 all-gather.8
  1882.5 38.9 reduce-scatter.3
